TPU v7x, 32 devices: a whole 2x2x4 slice. The times are simulated.
32 devices in a mesh: dp: 4 (over y, core), fsdp: 8 (over z, x).
Axes of the slice: x: 2, y: 2, z: 4, core: 2. Of those that a mesh axis runs over, the one named last changes fastest.
Arguments:
- block_input: bfloat16 [2, 16384, 1024], P(None, ('dp', 'fsdp'))
- cotangent: bfloat16 [2, 16384, 1024], P(None, ('dp', 'fsdp')), may hold values from -6 to 6
- query_weight: bfloat16 [1024, 1024], P(('dp', 'fsdp')), may hold values from -0.1875 to 0.1875
- key_weight: bfloat16 [1024, 1024], P(('dp', 'fsdp')), may hold values from -0.1875 to 0.1875
- value_weight: bfloat16 [1024, 1024], P(('dp', 'fsdp')), may hold values from -0.1875 to 0.1875
- gate_weight: bfloat16 [1024, 1024], P(('dp', 'fsdp')), may hold values from -0.1875 to 0.1875
- out_weight: bfloat16 [1024, 1024], P(('dp', 'fsdp')), may hold values from -0.1875 to 0.1875
- first_glu: bfloat16 [1024, 2816], P(('dp', 'fsdp')), may hold values from -0.1875 to 0.1875
- second_glu: bfloat16 [1024, 2816], P(('dp', 'fsdp')), may hold values from -0.1875 to 0.1875
- down_weight: bfloat16 [2816, 1024], P(('dp', 'fsdp')), may hold values from -0.109375 to 0.109375
- seq_lengths: int32 [2, 32, 4], P(None, ('dp', 'fsdp')), may hold values from 1 to 384, 512 in all within a row
- slot_index: int32 [2, 16384], P(None, ('dp', 'fsdp')), may hold values from 0 to 4095, as said below
Outputs:
- block_output: bfloat16 [2, 16384, 1024], P(None, ('dp', 'fsdp'))
- input_grad: bfloat16 [2, 16384, 1024], P(None, ('dp', 'fsdp'))
- query_grad: float32 [1024, 1024], P(('dp', 'fsdp'))
- key_grad: float32 [1024, 1024], P(('dp', 'fsdp'))
- value_grad: float32 [1024, 1024], P(('dp', 'fsdp'))
- gate_grad: float32 [1024, 1024], P(('dp', 'fsdp'))
- out_grad: float32 [1024, 1024], P(('dp', 'fsdp'))
- first_grad: float32 [1024, 2816], P(('dp', 'fsdp'))
- second_grad: float32 [1024, 2816], P(('dp', 'fsdp'))
- down_grad: float32 [2816, 1024], P(('dp', 'fsdp'))
- stream_rms: float32 [3], replicated
Inputs may be any that keep to these rules, and one draw needn't show every extreme that they name: `slot_index`: within each micro-batch and each aligned block of 4096 rows along the token dimension, the entries are a permutation of the group's slots; the 512 rows of one device name exactly 64 slots in each block of the group.
All inputs are finite; a program needn't handle non-finite values.
Results may differ from a plain program's by a relative error of at most 0.014.
Values may be sent and summed in bfloat16 or wider, within the bound.
A program may use at most 256 MiB of HBM per device.

v0:
```python
import math

import jax
import jax.numpy as jnp
from jax import lax
from jax.sharding import PartitionSpec as P

HEADS = 8
HEAD_DIM = 128
NSEG = 4


EPS = 1e-06


def rms_norm(vector):
    return vector * lax.rsqrt(jnp.mean(vector * vector, axis=-1, keepdims=True) + EPS)


def norm_back(vector, grad_in):
    inv_rms = lax.rsqrt(jnp.mean(vector * vector, axis=-1, keepdims=True) + EPS)
    unit_rows = vector * inv_rms
    return inv_rms * (grad_in - unit_rows * jnp.mean(grad_in * unit_rows, axis=-1, keepdims=True))


def swish_act(vector):
    return vector * jax.nn.sigmoid(vector)


def swish_slope(vector):
    sigmoid_val = jax.nn.sigmoid(vector)
    return sigmoid_val + vector * sigmoid_val * (1.0 - sigmoid_val)


def against(grad_rows, matrix):
    return lax.dot_general(
        grad_rows, matrix, (((1,), (1,)), ((), ())), preferred_element_type=jnp.float32
    )


def outer_sum(left, right):
    return lax.dot_general(
        left, right, (((0,), (0,)), ((), ())), preferred_element_type=jnp.float32
    )


def matmul(left, right):
    return jnp.dot(left, right, preferred_element_type=jnp.float32)


def block_frame(block_lengths, slot_count):
    seg_ends = jnp.cumsum(block_lengths)
    starts = seg_ends - block_lengths
    places = jnp.arange(slot_count, dtype=jnp.int32)
    member = (places[:, None] >= starts[None, :]) & (places[:, None] < seg_ends[None, :])
    segment = jnp.sum(jnp.where(member, jnp.arange(NSEG, dtype=jnp.int32)[None, :], 0), axis=1)
    offset = jnp.sum(jnp.where(member, starts[None, :], 0), axis=1)
    position = places - offset
    valid_rows = (places < seg_ends[NSEG - 2]).astype(jnp.float32)
    distance = places[:, None] - places[None, :]
    linked = (segment[:, None] == segment[None, :]) & (distance >= 0)
    head_ids = jnp.arange(HEADS, dtype=jnp.float32)
    log_decay = -jnp.exp2(-(head_ids + 1.0) * 8.0 / HEADS)
    steps_back = jnp.maximum(distance, 0).astype(jnp.float32)
    decay_mat = jnp.where(linked[None], jnp.exp(log_decay[:, None, None] * steps_back[None]), 0.0)
    frequency = jnp.exp(-math.log(10000.0) * jnp.arange(HEAD_DIM, dtype=jnp.float32) / HEAD_DIM)
    angles = position.astype(jnp.float32)[:, None] * frequency[None, :]
    return (jnp.cos(angles), jnp.sin(angles), decay_mat, valid_rows)


def rotate(vector, cosine, sine_vals):
    return jnp.concatenate([vector * cosine[:, None, :], vector * sine_vals[:, None, :]], axis=-1)


def unrotate(grad_rot, cosine, sine_vals, pre_act):
    row_count = grad_rot.shape[0]
    folded = (
        grad_rot[..., :HEAD_DIM] * cosine[:, None, :]
        + grad_rot[..., HEAD_DIM:] * sine_vals[:, None, :]
    )
    return (folded.reshape(row_count, HEADS * HEAD_DIM) * swish_slope(pre_act)).astype(jnp.bfloat16)


def forward_pass(stream_in, gathered, layout):
    query_mat, key_mat, value_mat, gate_mat, out_mat, first_mat, second_mat, down_mat = gathered
    cosine, sine_vals, decay_mat, valid_rows = layout
    row_count = stream_in.shape[0]
    normed_in = rms_norm(stream_in).astype(jnp.bfloat16)
    query_pre = matmul(normed_in, query_mat)
    key_pre = matmul(normed_in, key_mat)
    value_pre = matmul(normed_in, value_mat)
    gate_pre = matmul(normed_in, gate_mat)
    query_rot = rotate(
        swish_act(query_pre).reshape(row_count, HEADS, HEAD_DIM), cosine, sine_vals
    ).astype(jnp.bfloat16)
    key_rot = rotate(
        swish_act(key_pre).reshape(row_count, HEADS, HEAD_DIM), cosine, sine_vals
    ).astype(jnp.bfloat16)
    value_heads = value_pre.astype(jnp.bfloat16).reshape(row_count, HEADS, HEAD_DIM)
    scores = jnp.einsum("thc,shc->hts", query_rot, key_rot, preferred_element_type=jnp.float32)
    probs = (scores * decay_mat).astype(jnp.bfloat16)
    mixed = jnp.einsum(
        "hts,shc->thc", probs, value_heads, preferred_element_type=jnp.float32
    ).reshape(row_count, HEADS * HEAD_DIM)
    mixed_unit = rms_norm(mixed)
    gated = (mixed_unit * gate_pre).astype(jnp.bfloat16)
    attn_out = matmul(gated, out_mat)
    stream = stream_in + attn_out
    normed_mid = rms_norm(stream).astype(jnp.bfloat16)
    first = matmul(normed_mid, first_mat)
    second = matmul(normed_mid, second_mat)
    product = (first * second).astype(jnp.bfloat16)
    glu_out = matmul(product, down_mat)
    result = (stream + glu_out) * valid_rows[:, None]
    square_sums = jnp.stack(
        [
            jnp.sum(result * result),
            jnp.sum(attn_out * attn_out * valid_rows[:, None]),
            jnp.sum(glu_out * glu_out * valid_rows[:, None]),
        ]
    )
    stored = (
        stream_in,
        normed_in,
        query_pre,
        key_pre,
        gate_pre,
        query_rot,
        key_rot,
        value_heads,
        mixed,
        mixed_unit,
        gated,
        stream,
        normed_mid,
        first,
        second,
        product,
    )
    return (result, square_sums, stored)


def backward_pass(grad_in, gathered, layout, stored):
    query_mat, key_mat, value_mat, gate_mat, out_mat, first_mat, second_mat, down_mat = gathered
    cosine, sine_vals, decay_mat, valid_rows = layout
    (
        stream_in,
        normed_in,
        query_pre,
        key_pre,
        gate_pre,
        query_rot,
        key_rot,
        value_heads,
        mixed,
        mixed_unit,
        gated,
        stream,
        normed_mid,
        first,
        second,
        product,
    ) = stored
    row_count = stream_in.shape[0]
    grad_out = grad_in * valid_rows[:, None]
    grad_glu = grad_out.astype(jnp.bfloat16)
    down_part = outer_sum(product, grad_glu)
    grad_product = against(grad_glu, down_mat)
    grad_first = (grad_product * second).astype(jnp.bfloat16)
    grad_second = (grad_product * first).astype(jnp.bfloat16)
    first_part = outer_sum(normed_mid, grad_first)
    second_part = outer_sum(normed_mid, grad_second)
    grad_normed = against(grad_first, first_mat) + against(grad_second, second_mat)
    grad_stream = grad_out + norm_back(stream, grad_normed)
    grad_attn = grad_stream.astype(jnp.bfloat16)
    out_part = outer_sum(gated, grad_attn)
    grad_gated = against(grad_attn, out_mat)
    grad_gate = (grad_gated * mixed_unit).astype(jnp.bfloat16)
    grad_mixed = (
        norm_back(mixed, grad_gated * gate_pre)
        .astype(jnp.bfloat16)
        .reshape(row_count, HEADS, HEAD_DIM)
    )
    scores = jnp.einsum("thc,shc->hts", query_rot, key_rot, preferred_element_type=jnp.float32)
    probs = (scores * decay_mat).astype(jnp.bfloat16)
    grad_value = (
        jnp.einsum("hts,thc->shc", probs, grad_mixed, preferred_element_type=jnp.float32)
        .astype(jnp.bfloat16)
        .reshape(row_count, HEADS * HEAD_DIM)
    )
    grad_probs = jnp.einsum(
        "thc,shc->hts", grad_mixed, value_heads, preferred_element_type=jnp.float32
    )
    grad_scores = (grad_probs * decay_mat).astype(jnp.bfloat16)
    grad_qrot = jnp.einsum("hts,shc->thc", grad_scores, key_rot, preferred_element_type=jnp.float32)
    grad_krot = jnp.einsum(
        "hts,thc->shc", grad_scores, query_rot, preferred_element_type=jnp.float32
    )
    grad_query = unrotate(grad_qrot, cosine, sine_vals, query_pre)
    grad_key = unrotate(grad_krot, cosine, sine_vals, key_pre)
    query_part = outer_sum(normed_in, grad_query)
    key_part = outer_sum(normed_in, grad_key)
    value_part = outer_sum(normed_in, grad_value)
    gate_part = outer_sum(normed_in, grad_gate)
    grad_normed_in = (
        against(grad_query, query_mat)
        + against(grad_key, key_mat)
        + against(grad_value, value_mat)
        + against(grad_gate, gate_mat)
    )
    grad_rows = grad_stream + norm_back(stream_in, grad_normed_in)
    return (
        grad_rows,
        (query_part, key_part, value_part, gate_part, out_part, first_part, second_part, down_part),
    )


def body(
    block_input,
    cotangent,
    query_weight,
    key_weight,
    value_weight,
    gate_weight,
    out_weight,
    first_glu,
    second_glu,
    down_weight,
    seq_lengths,
    slot_index,
):
    peer_count = lax.axis_size("fsdp")
    micro_count, slot_count, model_width = block_input.shape
    per_peer = slot_count // peer_count
    shards = (
        query_weight,
        key_weight,
        value_weight,
        gate_weight,
        out_weight,
        first_glu,
        second_glu,
        down_weight,
    )
    send_orders = jnp.argsort(slot_index, axis=1)
    sorted_slots = jnp.take_along_axis(slot_index, send_orders, axis=1) % slot_count
    landing = lax.all_to_all(
        sorted_slots.reshape(micro_count, peer_count, per_peer),
        "fsdp",
        split_axis=1,
        concat_axis=1,
        tiled=True,
    )
    landing = landing.reshape(micro_count, slot_count)
    totals = tuple(
        (
            jnp.zeros((shard.shape[0] * lax.axis_size(("dp", "fsdp")), shard.shape[1]), jnp.float32)
            for shard in shards
        )
    )
    square_total = jnp.zeros((3,), jnp.float32)
    valid_count = jnp.zeros((), jnp.float32)
    out_list = []
    grad_list = []
    for batch_step in range(micro_count):
        send_order = send_orders[batch_step]
        slot_of = landing[batch_step]
        arrive = jnp.argsort(slot_of)
        send_rows = block_input[batch_step][send_order].reshape(peer_count, per_peer, model_width)
        send_grads = cotangent[batch_step][send_order].reshape(peer_count, per_peer, model_width)
        got_rows, got_grads = (
            lax.all_to_all(send_rows, "fsdp", split_axis=0, concat_axis=0, tiled=True),
            lax.all_to_all(send_grads, "fsdp", split_axis=0, concat_axis=0, tiled=True),
        )
        stream_in = got_rows.reshape(slot_count, model_width)[arrive].astype(jnp.float32)
        grad_in = got_grads.reshape(slot_count, model_width)[arrive].astype(jnp.float32)
        gathered = (
            lax.all_gather(query_weight, ("dp", "fsdp"), axis=0, tiled=True),
            lax.all_gather(key_weight, ("dp", "fsdp"), axis=0, tiled=True),
            lax.all_gather(value_weight, ("dp", "fsdp"), axis=0, tiled=True),
            lax.all_gather(gate_weight, ("dp", "fsdp"), axis=0, tiled=True),
            lax.all_gather(out_weight, ("dp", "fsdp"), axis=0, tiled=True),
            lax.all_gather(first_glu, ("dp", "fsdp"), axis=0, tiled=True),
            lax.all_gather(second_glu, ("dp", "fsdp"), axis=0, tiled=True),
            lax.all_gather(down_weight, ("dp", "fsdp"), axis=0, tiled=True),
        )
        layout = block_frame(seq_lengths[batch_step, 0], slot_count)
        result, square_sums, stored = forward_pass(stream_in, gathered, layout)
        again = (
            lax.all_gather(query_weight, ("dp", "fsdp"), axis=0, tiled=True),
            lax.all_gather(key_weight, ("dp", "fsdp"), axis=0, tiled=True),
            lax.all_gather(value_weight, ("dp", "fsdp"), axis=0, tiled=True),
            lax.all_gather(gate_weight, ("dp", "fsdp"), axis=0, tiled=True),
            lax.all_gather(out_weight, ("dp", "fsdp"), axis=0, tiled=True),
            lax.all_gather(first_glu, ("dp", "fsdp"), axis=0, tiled=True),
            lax.all_gather(second_glu, ("dp", "fsdp"), axis=0, tiled=True),
            lax.all_gather(down_weight, ("dp", "fsdp"), axis=0, tiled=True),
        )
        grad_rows, mat_grads = backward_pass(grad_in, again, layout, stored)
        totals = tuple((total + piece for total, piece in zip(totals, mat_grads)))
        square_total = square_total + square_sums
        valid_count = valid_count + jnp.sum(layout[3])
        reply_rows = result.astype(jnp.bfloat16)[slot_of].reshape(peer_count, per_peer, model_width)
        reply_grads = grad_rows.astype(jnp.bfloat16)[slot_of].reshape(
            peer_count, per_peer, model_width
        )
        back_rows, back_grads = (
            lax.all_to_all(reply_rows, "fsdp", split_axis=0, concat_axis=0, tiled=True),
            lax.all_to_all(reply_grads, "fsdp", split_axis=0, concat_axis=0, tiled=True),
        )
        restore = jnp.argsort(send_order)
        out_list.append(back_rows.reshape(slot_count, model_width)[restore])
        grad_list.append(back_grads.reshape(slot_count, model_width)[restore])
    totals = (
        lax.psum_scatter(totals[0], ("dp", "fsdp"), scatter_dimension=0, tiled=True),
        lax.psum_scatter(totals[1], ("dp", "fsdp"), scatter_dimension=0, tiled=True),
        lax.psum_scatter(totals[2], ("dp", "fsdp"), scatter_dimension=0, tiled=True),
        lax.psum_scatter(totals[3], ("dp", "fsdp"), scatter_dimension=0, tiled=True),
        lax.psum_scatter(totals[4], ("dp", "fsdp"), scatter_dimension=0, tiled=True),
        lax.psum_scatter(totals[5], ("dp", "fsdp"), scatter_dimension=0, tiled=True),
        lax.psum_scatter(totals[6], ("dp", "fsdp"), scatter_dimension=0, tiled=True),
        lax.psum_scatter(totals[7], ("dp", "fsdp"), scatter_dimension=0, tiled=True),
    )
    total_sums, total_count = lax.psum((square_total, valid_count), ("dp", "fsdp"))
    stream_rms = jnp.sqrt(total_sums / (total_count * model_width))
    return (
        jnp.stack(out_list),
        jnp.stack(grad_list),
        totals[0],
        totals[1],
        totals[2],
        totals[3],
        totals[4],
        totals[5],
        totals[6],
        totals[7],
        stream_rms,
    )


def solution(mesh):
    in_specs = (
        P(None, ("dp", "fsdp"), None),
        P(None, ("dp", "fsdp"), None),
        P(("dp", "fsdp"), None),
        P(("dp", "fsdp"), None),
        P(("dp", "fsdp"), None),
        P(("dp", "fsdp"), None),
        P(("dp", "fsdp"), None),
        P(("dp", "fsdp"), None),
        P(("dp", "fsdp"), None),
        P(("dp", "fsdp"), None),
        P(None, ("dp", "fsdp"), None),
        P(None, ("dp", "fsdp")),
    )
    out_specs = (
        P(None, ("dp", "fsdp"), None),
        P(None, ("dp", "fsdp"), None),
        P(("dp", "fsdp"), None),
        P(("dp", "fsdp"), None),
        P(("dp", "fsdp"), None),
        P(("dp", "fsdp"), None),
        P(("dp", "fsdp"), None),
        P(("dp", "fsdp"), None),
        P(("dp", "fsdp"), None),
        P(("dp", "fsdp"), None),
        P(),
    )
    return jax.shard_map(body, mesh=mesh, in_specs=in_specs, out_specs=out_specs, check_vma=False)
```

profile of v0, /device:TPU:0, one launch (start us, length us, event | category | flops | bytes accessed | tf_op | source)
XLA Modules:
  0.0 2152.0 jit_solution(13990540749734673434)
XLA Ops:
  15.8 9.1 gather_fusion.16
  25.8 7.3 all-to-all-start.1
  45.8 29.2 %all-to-all-done = bf16[8,64,1024]{2,1,0:T(8,128)(2,1)S(1)} async-done(((bf16[8,64,1024]{2,1,0:T(8,128)(2,1)}), bf16[8,64,1024]{2,1,0:T(8,128)(2,1)S(1)}, u32[]{:S(2)}, u32[]{:S(2)}) %all-to-all-start) | async-done | bytes 1048608 | tf_op jit(solution)/shard_map/all_to_all | solution.py:272
  84.1 21.7 %all-to-all-done.3 = bf16[8,64,1024]{2,1,0:T(8,128)(2,1)S(1)} async-done(((bf16[8,64,1024]{2,1,0:T(8,128)(2,1)}), bf16[8,64,1024]{2,1,0:T(8,128)(2,1)S(1)}, u32[]{:S(2)}, u32[]{:S(2)}) %all-to-all-start.3) | async-done | bytes 1048608 | tf_op jit(solution)/shard_map/all_to_all | solution.py:272
  115.2 4.8 gather_fusion.12
  120.0 21.5 all-to-all-done.5
  161.9 4.8 gather_fusion.9
  185.5 23.8 %all-gather.13.cloned.1.call-done = bf16[1024,1024]{1,0:T(8,128)(2,1)} async-done(((bf16[32,1024]{1,0:T(8,128)(2,1)}), bf16[1024,1024]{1,0:T(8,128)(2,1)}) %all-gather.13.cloned.1.call-update) | async-done | bytes 2097168 | tf_op jit(solution)/shard_map/all_gather | solution.py:279
  239.5 28.2 %all-gather.15.cloned.1.call-done = bf16[1024,1024]{1,0:T(8,128)(2,1)} async-done(((bf16[32,1024]{1,0:T(8,128)(2,1)}), bf16[1024,1024]{1,0:T(8,128)(2,1)}) %all-gather.15.cloned.1.call-update) | async-done | bytes 2097168 | tf_op jit(solution)/shard_map/all_gather | solution.py:281
  267.7 5.2 multiply_convert_fusion.14
  272.8 53.1 %all-gather.17.cloned.1.call-done = bf16[1024,1024]{1,0:T(8,128)(2,1)} async-done(((bf16[32,1024]{1,0:T(8,128)(2,1)}), bf16[1024,1024]{1,0:T(8,128)(2,1)}) %all-gather.17.cloned.1.call-update) | async-done | bytes 2097168 | tf_op jit(solution)/shard_map/all_gather | solution.py:282
  325.9 4.7 multiply_reduce_fusion.10
  339.0 55.9 %all-gather.21.cloned.1.call-done = bf16[1024,2816]{1,0:T(8,128)(2,1)} async-done(((bf16[32,2816]{1,0:T(8,128)(2,1)}), bf16[1024,2816]{1,0:T(8,128)(2,1)}) %all-gather.21.cloned.1.call-update) | async-done | bytes 5767184 | tf_op jit(solution)/shard_map/all_gather | solution.py:284
  394.9 8.6 fusion.125
  403.6 59.9 %all-gather.19.cloned.1.call-done = bf16[1024,2816]{1,0:T(8,128)(2,1)} async-done(((bf16[32,2816]{1,0:T(8,128)(2,1)}), bf16[1024,2816]{1,0:T(8,128)(2,1)}) %all-gather.19.cloned.1.call-update) | async-done | bytes 5767184 | tf_op jit(solution)/shard_map/all_gather | solution.py:283
  463.5 8.5 fusion.124
  472.0 60.0 %all-gather.23.cloned.1.call-done = bf16[2816,1024]{1,0:T(8,128)(2,1)} async-done(((bf16[88,1024]{1,0:T(8,128)(2,1)}), bf16[2816,1024]{1,0:T(8,128)(2,1)}) %all-gather.23.cloned.1.call-update) | async-done | bytes 5767184 | tf_op jit(solution)/shard_map/all_gather | solution.py:285
  532.0 11.6 multiply_convert_fusion.6
  543.7 7.3 fusion.128
  551.1 5.4 convolution_add_fusion.9
  556.5 5.4 multiply_reduce_fusion.5
  578.8 5.0 fusion.127
  583.7 5.2 fusion.126
  588.9 8.7 multiply_convert_fusion.4
  597.6 6.2 fusion.132
  603.9 5.4 convolution_add_fusion.8
  609.3 5.6 multiply_reduce_fusion.2
  684.4 5.5 fusion.74
  689.9 6.1 convolution_add_fusion
  696.1 5.6 fusion.137
  701.7 6.2 convolution_add_fusion.1
  708.0 5.6 fusion.136
  713.6 6.3 convolution_add_fusion.2
  738.5 4.9 gather_fusion.10
  743.3 16.1 all-to-all-done.2
  763.3 4.8 gather_fusion.6
  772.7 20.6 all-to-all-done.6
  806.8 4.8 gather_fusion.14
  811.6 18.2 all-to-all-done.4
  848.6 46.1 %all-reduce = (f32[3]{0:T(128)S(1)}, f32[]{:T(128)}) all-reduce(f32[3]{0:T(128)S(1)} %maximum_add_fusion, f32[]{:T(128)S(6)} %add.332), channel_id=1, replica_groups=mesh['dp'=4,'fsdp'=8] {'dp','fsdp'}, use_global_device_ids=true, to_apply=%region_37.38 | all-reduce | flops 4 | bytes 32 | tf_op jit(solution)/shard_map/psum | solution.py:324
  900.6 4.8 gather_fusion.7
  912.6 44.0 %reduce-scatter.15.cloned.1.call-done = f32[32,1024]{1,0:T(8,128)} async-done(((f32[1024,1024]{1,0:T(8,128)}), f32[32,1024]{1,0:T(8,128)}) %reduce-scatter.15.cloned.1.call-update) | async-done | bytes 131088 | tf_op jit(solution)/shard_map/reduce_scatter | solution.py:318
  956.6 144.2 %reduce-scatter.17.cloned.1.call-done = f32[32,1024]{1,0:T(8,128)} async-done(((f32[1024,1024]{1,0:T(8,128)}), f32[32,1024]{1,0:T(8,128)}) %reduce-scatter.17.cloned.1.call-update) | async-done | bytes 131088 | tf_op jit(solution)/shard_map/reduce_scatter | solution.py:319
  1100.8 145.9 %reduce-scatter.9.cloned.1.call-done = f32[32,1024]{1,0:T(8,128)} async-done(((f32[1024,1024]{1,0:T(8,128)}), f32[32,1024]{1,0:T(8,128)}) %reduce-scatter.9.cloned.1.call-update) | async-done | bytes 131088 | tf_op jit(solution)/shard_map/reduce_scatter | solution.py:315
  1246.7 144.8 %reduce-scatter.11.cloned.1.call-done = f32[32,1024]{1,0:T(8,128)} async-done(((f32[1024,1024]{1,0:T(8,128)}), f32[32,1024]{1,0:T(8,128)}) %reduce-scatter.11.cloned.1.call-update) | async-done | bytes 131088 | tf_op jit(solution)/shard_map/reduce_scatter | solution.py:316
  1391.5 250.1 %reduce-scatter.23.cloned.1.call-done = f32[88,1024]{1,0:T(8,128)} async-done(((f32[2816,1024]{1,0:T(8,128)}), f32[88,1024]{1,0:T(8,128)}) %reduce-scatter.23.cloned.1.call-update) | async-done | bytes 360464 | tf_op jit(solution)/shard_map/reduce_scatter | solution.py:322
  1641.6 251.3 %reduce-scatter.21.cloned.1.call-done = f32[32,2816]{1,0:T(8,128)} async-done(((f32[1024,2816]{1,0:T(8,128)}), f32[32,2816]{1,0:T(8,128)}) %reduce-scatter.21.cloned.1.call-update) | async-done | bytes 360464 | tf_op jit(solution)/shard_map/reduce_scatter | solution.py:321
  1892.9 251.3 %reduce-scatter.19.cloned.1.call-done = f32[32,2816]{1,0:T(8,128)} async-done(((f32[1024,2816]{1,0:T(8,128)}), f32[32,2816]{1,0:T(8,128)}) %reduce-scatter.19.cloned.1.call-update) | async-done | bytes 360464 | tf_op jit(solution)/shard_map/reduce_scatter | solution.py:320
  (437 shorter events, 272.9 us)
Async XLA Ops:
  8.0 7.1 sort.82.cloned.1.call-start
  8.7 168.7 %all-gather.9.cloned.1.call-start = ((), (), s32[]{:S(2)}) async-start(), calls=%async_computation.17 | async-start | bytes 2162688 | tf_op jit(solution)/shard_map/all_gather | solution.py:280
  9.3 172.0 %all-gather.11.cloned.1.call-start = ((), (), s32[]{:S(2)}) async-start(), calls=%async_computation.18 | async-start | bytes 2162688 | tf_op jit(solution)/shard_map/all_gather | solution.py:278
  9.9 199.5 %all-gather.13.cloned.1.call-start = ((), (), s32[]{:S(2)}) async-start(), calls=%async_computation.19 | async-start | bytes 2162688 | tf_op jit(solution)/shard_map/all_gather | solution.py:279
  10.5 257.2 %all-gather.15.cloned.1.call-start = ((), (), s32[]{:S(2)}) async-start(), calls=%async_computation.20 | async-start | bytes 2162688 | tf_op jit(solution)/shard_map/all_gather | solution.py:281
  11.2 314.7 %all-gather.17.cloned.1.call-start = ((), (), s32[]{:S(2)}) async-start(), calls=%async_computation.21 | async-start | bytes 2162688 | tf_op jit(solution)/shard_map/all_gather | solution.py:282
  12.0 382.9 %all-gather.21.cloned.1.call-start = ((), (), s32[]{:S(2)}) async-start(), calls=%async_computation.23 | async-start | bytes 5947392 | tf_op jit(solution)/shard_map/all_gather | solution.py:284
  12.7 450.8 %all-gather.19.cloned.1.call-start = ((), (), s32[]{:S(2)}) async-start(), calls=%async_computation.22 | async-start | bytes 5947392 | tf_op jit(solution)/shard_map/all_gather | solution.py:283
  15.8 9.1 copy-start.97
  25.8 13.7 all-to-all-start.1
  39.5 35.6 %all-to-all-start = ((bf16[8,64,1024]{2,1,0:T(8,128)(2,1)}), bf16[8,64,1024]{2,1,0:T(8,128)(2,1)S(1)}, u32[]{:S(2)}, u32[]{:S(2)}) async-start(bf16[8,64,1024]{2,1,0:T(8,128)(2,1)} %bitcast.3), calls=%async_computation | async-start | bytes 2097152 | tf_op jit(solution)/shard_map/all_to_all | solution.py:272
  75.1 30.8 %all-to-all-start.3 = ((bf16[8,64,1024]{2,1,0:T(8,128)(2,1)}), bf16[8,64,1024]{2,1,0:T(8,128)(2,1)S(1)}, u32[]{:S(2)}, u32[]{:S(2)}) async-start(bf16[8,64,1024]{2,1,0:T(8,128)(2,1)} %bitcast.285), calls=%async_computation.3 | async-start | bytes 2097152 | tf_op jit(solution)/shard_map/all_to_all | solution.py:272
  84.1 26.0 %copy-start.101 = (s32[2,1,4]{2,1,0:T(1,128)S(1)}, s32[2,1,4]{2,1,0:T(1,128)}, u32[]{:S(2)}) copy-start(s32[2,1,4]{2,1,0:T(1,128)} %param.22) | copy-start | bytes 100
  105.8 35.6 %all-to-all-start.5 = ((bf16[8,64,1024]{2,1,0:T(8,128)(2,1)}), bf16[8,64,1024]{2,1,0:T(8,128)(2,1)S(1)}, u32[]{:S(2)}, u32[]{:S(2)}) async-start(bf16[8,64,1024]{2,1,0:T(8,128)(2,1)} %bitcast.281), calls=%async_computation.5 | async-start | bytes 2097152 | tf_op jit(solution)/shard_map/all_to_all | solution.py:273
  109.5 422.5 %all-gather.23.cloned.1.call-start = ((), (), s32[]{:S(2)}) async-start(), calls=%async_computation.24 | async-start | bytes 5947392 | tf_op jit(solution)/shard_map/all_gather | solution.py:285
  141.5 18.4 copy-start.1
  141.5 31.8 %all-to-all-start.7 = ((bf16[8,64,1024]{2,1,0:T(8,128)(2,1)}), bf16[8,64,1024]{2,1,0:T(8,128)(2,1)}, u32[]{:S(2)}, u32[]{:S(2)}) async-start(bf16[8,64,1024]{2,1,0:T(8,128)(2,1)} %bitcast.279), calls=%async_computation.7 | async-start | bytes 2097152 | tf_op jit(solution)/shard_map/all_to_all | solution.py:273
  145.8 766.8 %reduce-scatter.13.cloned.1.call-start = ((), (), s32[]{:S(2)}) async-start(), calls=%async_computation.27 | async-start | bytes 4325376 | tf_op jit(solution)/shard_map/reduce_scatter | solution.py:317
  150.2 78.9 %copy-start.68 = (f32[512,128]{1,0:T(8,128)}, f32[512,128]{1,0:T(8,128)S(1)}, u32[]{:S(2)}) copy-start(f32[512,128]{1,0:T(8,128)S(1)} %get-tuple-element.89) | copy-start | bytes 786436
  225.8 7.7 copy-start.90
  330.6 5.6 copy-start.38
  543.7 7.4 copy-start.65
  543.7 7.4 copy-start.66
  543.7 12.8 slice-start
  551.0 5.4 slice-start.1
  556.5 5.4 copy-start.29
  562.6 5.4 copy-start.6
  571.7 7.0 slice-start.4
  575.1 8.6 slice-start.6
  578.7 10.1 slice-start.2
  597.6 6.2 copy-start.23
  632.7 324.0 %reduce-scatter.15.cloned.1.call-start = ((), (), s32[]{:S(2)}) async-start(), calls=%async_computation.28 | async-start | bytes 4325376 | tf_op jit(solution)/shard_map/reduce_scatter | solution.py:318
  638.9 461.9 %reduce-scatter.17.cloned.1.call-start = ((), (), s32[]{:S(2)}) async-start(), calls=%async_computation.29 | async-start | bytes 4325376 | tf_op jit(solution)/shard_map/reduce_scatter | solution.py:319
  645.8 600.9 %reduce-scatter.9.cloned.1.call-start = ((), (), s32[]{:S(2)}) async-start(), calls=%async_computation.25 | async-start | bytes 4325376 | tf_op jit(solution)/shard_map/reduce_scatter | solution.py:315
  673.3 718.3 %reduce-scatter.11.cloned.1.call-start = ((), (), s32[]{:S(2)}) async-start(), calls=%async_computation.26 | async-start | bytes 4325376 | tf_op jit(solution)/shard_map/reduce_scatter | solution.py:316
  684.1 957.4 %reduce-scatter.23.cloned.1.call-start = ((), (), s32[]{:S(2)}) async-start(), calls=%async_computation.32 | async-start | bytes 11894784 | tf_op jit(solution)/shard_map/reduce_scatter | solution.py:322
  684.4 5.5 copy-start.15
  696.0 5.7 copy-start.21
  696.0 1196.8 %reduce-scatter.21.cloned.1.call-start = ((), (), s32[]{:S(2)}) async-start(), calls=%async_computation.31 | async-start | bytes 11894784 | tf_op jit(solution)/shard_map/reduce_scatter | solution.py:321
  696.1 5.6 copy-start.24
  708.0 1436.2 %reduce-scatter.19.cloned.1.call-start = ((), (), s32[]{:S(2)}) async-start(), calls=%async_computation.30 | async-start | bytes 11894784 | tf_op jit(solution)/shard_map/reduce_scatter | solution.py:320
  708.0 5.6 copy-start.22
  723.9 35.5 %all-to-all-start.2 = ((bf16[8,64,1024]{2,1,0:T(8,128)(2,1)}), bf16[8,64,1024]{2,1,0:T(8,128)(2,1)S(1)}, u32[]{:S(2)}, u32[]{:S(2)}) async-start(bf16[8,64,1024]{2,1,0:T(8,128)(2,1)} %bitcast.283), calls=%async_computation.2 | async-start | bytes 2097152 | tf_op jit(solution)/shard_map/all_to_all | solution.py:308
  743.3 19.9 copy-start.99
  759.4 33.9 %all-to-all-start.6 = ((bf16[8,64,1024]{2,1,0:T(8,128)(2,1)}), bf16[8,64,1024]{2,1,0:T(8,128)(2,1)S(1)}, u32[]{:S(2)}, u32[]{:S(2)}) async-start(bf16[8,64,1024]{2,1,0:T(8,128)(2,1)} %bitcast.284), calls=%async_computation.6 | async-start | bytes 2097152 | tf_op jit(solution)/shard_map/all_to_all | solution.py:309
  793.3 36.5 %all-to-all-start.4 = ((bf16[8,64,1024]{2,1,0:T(8,128)(2,1)}), bf16[8,64,1024]{2,1,0:T(8,128)(2,1)}, u32[]{:S(2)}, u32[]{:S(2)}) async-start(bf16[8,64,1024]{2,1,0:T(8,128)(2,1)} %bitcast.282), calls=%async_computation.4 | async-start | bytes 2097152 | tf_op jit(solution)/shard_map/all_to_all | solution.py:308
  811.6 25.6 %copy-start.98 = (s32[2,512]{1,0:T(2,128)S(1)}, s32[2,512]{1,0:T(2,128)}, u32[]{:S(2)}) copy-start(s32[2,512]{1,0:T(2,128)} %get-tuple-element.16) | copy-start | bytes 12292
  829.8 75.7 %all-to-all-start.8 = ((bf16[8,64,1024]{2,1,0:T(8,128)(2,1)}), bf16[8,64,1024]{2,1,0:T(8,128)(2,1)S(1)}, u32[]{:S(2)}, u32[]{:S(2)}) async-start(bf16[8,64,1024]{2,1,0:T(8,128)(2,1)} %bitcast.280), calls=%async_computation.8 | async-start | bytes 2097152 | tf_op jit(solution)/shard_map/all_to_all | solution.py:309
  (95 other events, 251.7 us)
Sparse Core Ops, SparseCore 0:
  11.8 3.0 sort.84.cloned.1.call-done
  (1 shorter events, 0.0 us)
Sparse Core Ops, SparseCore 1:
  12.2 64.5 all-gather.8
  79.7 65.7 all-gather.10
  148.3 61.0 all-gather.12
  212.4 55.2 all-gather.14
  270.7 55.2 all-gather.16
  328.9 66.0 all-gather.20
  397.7 65.7 all-gather.18
  466.3 65.7 all-gather.22
  632.8 160.6 reduce-scatter.12
  796.3 160.2 reduce-scatter.14
  959.4 141.4 reduce-scatter.16
  1103.7 142.9 reduce-scatter.8
  1249.4 142.1 reduce-scatter.10
  1394.4 247.1 reduce-scatter.22
  1644.5 248.3 reduce-scatter.20
  1895.8 248.4 reduce-scatter.18
where the time goes:
time: 2160 us; the launch traced here: 2150 us
  waiting for transfers between devices  1650 us (76%)
  matrix products  234 us (11%)
  local copies, waits for them, and re-layouts  102 us (5%)
  other arithmetic  57.9 us (3%)
  blocking collectives  46.1 us (2%)
  starting transfers between devices  40.2 us (2%)
    reduce_scatter x1, waiting for transfers between devices, body(): lax.psum_scatter(totals[5], ('dp', 'fsdp'), scatter_dimension=0, tiled=True)  251 us
    reduce_scatter x1, waiting for transfers between devices, body(): lax.psum_scatter(totals[6], ('dp', 'fsdp'), scatter_dimension=0, tiled=True)  251 us
    reduce_scatter x1, waiting for transfers between devices, body(): lax.psum_scatter(totals[7], ('dp', 'fsdp'), scatter_dimension=0, tiled=True)  250 us
    reduce_scatter x1, waiting for transfers between devices, body(): lax.psum_scatter(totals[0], ('dp', 'fsdp'), scatter_dimension=0, tiled=True)  146 us
    reduce_scatter x1, waiting for transfers between devices, body(): lax.psum_scatter(totals[1], ('dp', 'fsdp'), scatter_dimension=0, tiled=True)  145 us
    reduce_scatter x1, waiting for transfers between devices, body(): lax.psum_scatter(totals[4], ('dp', 'fsdp'), scatter_dimension=0, tiled=True)  144 us
    dot_general x16, matrix products, matmul(): return jnp.dot(left, right, preferred_element_type=jnp.float32)  70.5 us
    dot_general x16, matrix products, against(): lax.dot_general(grad_rows, matrix, (((1,), (1,)), ((), ())), preferred_el...  67.7 us
  transfers between devices with their start and end apart: 25, of which 21 were waited for; matrix products, arithmetic and copies ran while one was open for 13% of the time, Pallas kernels for 0%

commit v1 on v0

v1 whole, which is shorter than its diff:
```python
import math

import jax
import jax.numpy as jnp
from jax import lax
from jax.sharding import PartitionSpec as P

HEADS = 8
HEAD_DIM = 128
NSEG = 4


EPS = 1e-06


def rms_norm(vector):
    return vector * lax.rsqrt(jnp.mean(vector * vector, axis=-1, keepdims=True) + EPS)


def norm_back(vector, grad_in):
    inv_rms = lax.rsqrt(jnp.mean(vector * vector, axis=-1, keepdims=True) + EPS)
    unit_rows = vector * inv_rms
    return inv_rms * (grad_in - unit_rows * jnp.mean(grad_in * unit_rows, axis=-1, keepdims=True))


def swish_act(vector):
    return vector * jax.nn.sigmoid(vector)


def swish_slope(vector):
    sigmoid_val = jax.nn.sigmoid(vector)
    return sigmoid_val + vector * sigmoid_val * (1.0 - sigmoid_val)


def against(grad_rows, matrix):
    return lax.dot_general(
        grad_rows, matrix, (((1,), (1,)), ((), ())), preferred_element_type=jnp.float32
    )


def outer_sum(left, right):
    return lax.dot_general(
        left, right, (((0,), (0,)), ((), ())), preferred_element_type=jnp.float32
    )


def matmul(left, right):
    return jnp.dot(left, right, preferred_element_type=jnp.float32)


def block_frame(block_lengths, slot_count):
    seg_ends = jnp.cumsum(block_lengths)
    starts = seg_ends - block_lengths
    places = jnp.arange(slot_count, dtype=jnp.int32)
    member = (places[:, None] >= starts[None, :]) & (places[:, None] < seg_ends[None, :])
    segment = jnp.sum(jnp.where(member, jnp.arange(NSEG, dtype=jnp.int32)[None, :], 0), axis=1)
    offset = jnp.sum(jnp.where(member, starts[None, :], 0), axis=1)
    position = places - offset
    valid_rows = (places < seg_ends[NSEG - 2]).astype(jnp.float32)
    distance = places[:, None] - places[None, :]
    linked = (segment[:, None] == segment[None, :]) & (distance >= 0)
    head_ids = jnp.arange(HEADS, dtype=jnp.float32)
    log_decay = -jnp.exp2(-(head_ids + 1.0) * 8.0 / HEADS)
    steps_back = jnp.maximum(distance, 0).astype(jnp.float32)
    decay_mat = jnp.where(linked[None], jnp.exp(log_decay[:, None, None] * steps_back[None]), 0.0)
    frequency = jnp.exp(-math.log(10000.0) * jnp.arange(HEAD_DIM, dtype=jnp.float32) / HEAD_DIM)
    angles = position.astype(jnp.float32)[:, None] * frequency[None, :]
    return (jnp.cos(angles), jnp.sin(angles), decay_mat, valid_rows)


def rotate(vector, cosine, sine_vals):
    return jnp.concatenate([vector * cosine[:, None, :], vector * sine_vals[:, None, :]], axis=-1)


def unrotate(grad_rot, cosine, sine_vals, pre_act):
    row_count = grad_rot.shape[0]
    folded = (
        grad_rot[..., :HEAD_DIM] * cosine[:, None, :]
        + grad_rot[..., HEAD_DIM:] * sine_vals[:, None, :]
    )
    return (folded.reshape(row_count, HEADS * HEAD_DIM) * swish_slope(pre_act)).astype(jnp.bfloat16)


def sort_slots(slots, slot_count):
    rank = jnp.sum((slots[:, None, :] < slots[:, :, None]).astype(jnp.int32), axis=2)
    places = jnp.arange(slot_count, dtype=jnp.int32)
    hit = rank[:, None, :] == places[None, :, None]
    ordered = jnp.sum(jnp.where(hit, slots[:, None, :], 0), axis=2)
    return hit.astype(jnp.bfloat16), ordered


def pick(selector, rows):
    return jnp.einsum("mrs,msd->mrd", selector, rows, preferred_element_type=jnp.float32)


def put_back(selector, rows):
    return jnp.einsum("mrs,mrd->msd", selector, rows, preferred_element_type=jnp.float32)


def swap_rows(rows, peer_count):
    micro_count, slot_count, width = rows.shape
    split = rows.reshape(micro_count, peer_count, slot_count // peer_count, width)
    moved = lax.all_to_all(split, "fsdp", split_axis=1, concat_axis=1, tiled=True)
    return moved.reshape(micro_count, slot_count, width)


def gather_rows(shard):
    return lax.all_gather(shard, ("dp", "fsdp"), axis=0, tiled=True)


def scatter_sum(total):
    return lax.psum_scatter(total, ("dp", "fsdp"), scatter_dimension=0, tiled=True)


def body(
    block_input,
    cotangent,
    query_weight,
    key_weight,
    value_weight,
    gate_weight,
    out_weight,
    first_glu,
    second_glu,
    down_weight,
    seq_lengths,
    slot_index,
):
    peer_count = lax.axis_size("fsdp")
    micro_count, slot_count, width = block_input.shape
    ff_width = first_glu.shape[1]
    row_count = micro_count * slot_count

    front_mat = gather_rows(
        jnp.concatenate([query_weight, key_weight, value_weight, gate_weight], axis=1)
    )
    out_mat = gather_rows(out_weight)
    glu_mat = gather_rows(jnp.concatenate([first_glu, second_glu], axis=1))
    down_mat = gather_rows(down_weight)

    send_hit, ordered = sort_slots(slot_index, slot_count)
    landing = swap_rows((ordered % slot_count)[:, :, None], peer_count)[:, :, 0]
    both = jnp.concatenate([block_input, cotangent], axis=2)
    sent = pick(send_hit, both).astype(jnp.bfloat16)
    got = swap_rows(sent, peer_count)
    places = jnp.arange(slot_count, dtype=jnp.int32)
    land_hit = (landing[:, :, None] == places[None, None, :]).astype(jnp.bfloat16)
    slot_rows = put_back(land_hit, got)
    stream_in = slot_rows[:, :, :width].reshape(row_count, width)
    grad_in = slot_rows[:, :, width:].reshape(row_count, width)

    cosine, sine_vals, decay_mat, valid_rows = jax.vmap(
        lambda lengths: block_frame(lengths, slot_count)
    )(seq_lengths[:, 0])
    valid_rows = valid_rows.reshape(row_count)
    cosine = cosine.reshape(row_count, HEAD_DIM)
    sine_vals = sine_vals.reshape(row_count, HEAD_DIM)

    def heads(array):
        return array.reshape(micro_count, slot_count, HEADS, -1)

    normed_in = rms_norm(stream_in).astype(jnp.bfloat16)
    front = matmul(normed_in, front_mat)
    query_pre, key_pre, value_pre, gate_pre = (
        front[:, i * width : (i + 1) * width] for i in range(4)
    )
    query_rot = heads(
        rotate(swish_act(query_pre).reshape(row_count, HEADS, HEAD_DIM), cosine, sine_vals).astype(
            jnp.bfloat16
        )
    )
    key_rot = heads(
        rotate(swish_act(key_pre).reshape(row_count, HEADS, HEAD_DIM), cosine, sine_vals).astype(
            jnp.bfloat16
        )
    )
    value_heads = heads(value_pre.astype(jnp.bfloat16))
    scores = jnp.einsum("mthc,mshc->mhts", query_rot, key_rot, preferred_element_type=jnp.float32)
    probs = (scores * decay_mat).astype(jnp.bfloat16)
    mixed = jnp.einsum(
        "mhts,mshc->mthc", probs, value_heads, preferred_element_type=jnp.float32
    ).reshape(row_count, width)
    mixed_unit = rms_norm(mixed)
    gated = (mixed_unit * gate_pre).astype(jnp.bfloat16)
    attn_out = matmul(gated, out_mat)
    stream = stream_in + attn_out
    normed_mid = rms_norm(stream).astype(jnp.bfloat16)
    glu_in = matmul(normed_mid, glu_mat)
    first, second = glu_in[:, :ff_width], glu_in[:, ff_width:]
    product = (first * second).astype(jnp.bfloat16)
    glu_out = matmul(product, down_mat)
    result = (stream + glu_out) * valid_rows[:, None]
    square_sums = jnp.stack(
        [
            jnp.sum(result * result),
            jnp.sum(attn_out * attn_out * valid_rows[:, None]),
            jnp.sum(glu_out * glu_out * valid_rows[:, None]),
        ]
    )
    result_rows = result.astype(jnp.bfloat16)

    grad_out = grad_in * valid_rows[:, None]
    grad_glu = grad_out.astype(jnp.bfloat16)
    down_part = outer_sum(product, grad_glu).astype(jnp.bfloat16)
    grad_product = against(grad_glu, down_mat)
    grad_pair = jnp.concatenate(
        [
            (grad_product * second).astype(jnp.bfloat16),
            (grad_product * first).astype(jnp.bfloat16),
        ],
        axis=1,
    )
    glu_part = outer_sum(normed_mid, grad_pair).astype(jnp.bfloat16)
    grad_stream = grad_out + norm_back(stream, against(grad_pair, glu_mat))
    grad_attn = grad_stream.astype(jnp.bfloat16)
    out_part = outer_sum(gated, grad_attn).astype(jnp.bfloat16)
    grad_gated = against(grad_attn, out_mat)
    grad_gate = (grad_gated * mixed_unit).astype(jnp.bfloat16)
    grad_mixed = heads(norm_back(mixed, grad_gated * gate_pre).astype(jnp.bfloat16))
    grad_value = (
        jnp.einsum("mhts,mthc->mshc", probs, grad_mixed, preferred_element_type=jnp.float32)
        .astype(jnp.bfloat16)
        .reshape(row_count, width)
    )
    grad_probs = jnp.einsum(
        "mthc,mshc->mhts", grad_mixed, value_heads, preferred_element_type=jnp.float32
    )
    grad_scores = (grad_probs * decay_mat).astype(jnp.bfloat16)
    grad_qrot = jnp.einsum(
        "mhts,mshc->mthc", grad_scores, key_rot, preferred_element_type=jnp.float32
    ).reshape(row_count, HEADS, 2 * HEAD_DIM)
    grad_krot = jnp.einsum(
        "mhts,mthc->mshc", grad_scores, query_rot, preferred_element_type=jnp.float32
    ).reshape(row_count, HEADS, 2 * HEAD_DIM)
    grad_query = unrotate(grad_qrot, cosine, sine_vals, query_pre)
    grad_key = unrotate(grad_krot, cosine, sine_vals, key_pre)
    grad_front = jnp.concatenate([grad_query, grad_key, grad_value, grad_gate], axis=1)
    front_part = outer_sum(normed_in, grad_front).astype(jnp.bfloat16)
    grad_rows = grad_stream + norm_back(stream_in, against(grad_front, front_mat))

    replies = jnp.concatenate([result_rows, grad_rows.astype(jnp.bfloat16)], axis=1)
    replies = replies.reshape(micro_count, slot_count, 2 * width)
    back = swap_rows(pick(land_hit, replies).astype(jnp.bfloat16), peer_count)
    given = put_back(send_hit, back).astype(jnp.bfloat16)

    down_grad = scatter_sum(down_part).astype(jnp.float32)
    glu_grad = scatter_sum(glu_part).astype(jnp.float32)
    out_grad = scatter_sum(out_part).astype(jnp.float32)
    front_grad = scatter_sum(front_part).astype(jnp.float32)
    total_sums, total_count = lax.psum((square_sums, jnp.sum(valid_rows)), ("dp", "fsdp"))
    stream_rms = jnp.sqrt(total_sums / (total_count * width))
    return (
        given[:, :, :width],
        given[:, :, width:],
        front_grad[:, :width],
        front_grad[:, width : 2 * width],
        front_grad[:, 2 * width : 3 * width],
        front_grad[:, 3 * width :],
        out_grad,
        glu_grad[:, :ff_width],
        glu_grad[:, ff_width:],
        down_grad,
        stream_rms,
    )


def solution(mesh):
    in_specs = (
        P(None, ("dp", "fsdp"), None),
        P(None, ("dp", "fsdp"), None),
        P(("dp", "fsdp"), None),
        P(("dp", "fsdp"), None),
        P(("dp", "fsdp"), None),
        P(("dp", "fsdp"), None),
        P(("dp", "fsdp"), None),
        P(("dp", "fsdp"), None),
        P(("dp", "fsdp"), None),
        P(("dp", "fsdp"), None),
        P(None, ("dp", "fsdp"), None),
        P(None, ("dp", "fsdp")),
    )
    out_specs = (
        P(None, ("dp", "fsdp"), None),
        P(None, ("dp", "fsdp"), None),
        P(("dp", "fsdp"), None),
        P(("dp", "fsdp"), None),
        P(("dp", "fsdp"), None),
        P(("dp", "fsdp"), None),
        P(("dp", "fsdp"), None),
        P(("dp", "fsdp"), None),
        P(("dp", "fsdp"), None),
        P(("dp", "fsdp"), None),
        P(),
    )
    return jax.shard_map(body, mesh=mesh, in_specs=in_specs, out_specs=out_specs, check_vma=False)
```

time: 2160 us -> 1240 us (0.57)
  waiting for transfers between devices: 1650 us -> 681 us
  blocking collectives: 46.1 us -> 132 us
  local copies, waits for them, and re-layouts: 102 us -> 79 us
  starting transfers between devices: 40.2 us -> 18.4 us
    reduce_scatter x8 -> x4, waiting for transfers between devices: 1230 us -> 457 us  [scatter_sum(): lax.psum_scatter(total, ('dp', 'fsdp'), scatter_dimension=0, tiled=True)]
    all_gather x8 -> x4, waiting for transfers between devices: 281 us -> 110 us  [gather_rows(): return lax.all_gather(shard, ('dp', 'fsdp'), axis=0, tiled=True)]
    psum x1, blocking collectives: 46.1 us -> 132 us  [body(): lax.psum((square_sums, jnp.sum(valid_rows)), ('dp', 'fsdp'))]
    gather x18 -> x0, local copies, waits for them, and re-layouts: 65 us -> none  [the longest x2 9.69 us: body(): grad_rows.astype(jnp.bfloat16)[slot_of]]
    dot_general x12 -> x10, matrix products: 30.6 us -> 68.1 us  [the longest x1 10.4 us: body(): jnp.einsum('mhts,mshc->mthc', grad_scores, key_rot, preferred_element_typ...]
    transpose x0 -> x3, local copies, waits for them, and re-layouts: none -> 26 us  [the longest x1 10.4 us: body(): jnp.einsum('mhts,mthc->mshc', grad_scores, query_rot, preferred_element_t...]
    all_to_all x9 -> x3, waiting for transfers between devices: 135 us -> 114 us  [swap_rows(): lax.all_to_all(split, 'fsdp', split_axis=1, concat_axis=1, tiled=True)]
    dot_general x16 -> x4, matrix products: 64.9 us -> 50.2 us  [outer_sum(): lax.dot_general(left, right, (((0,), (0,)), ((), ())), preferred_element_...]
  transfers between devices with their start and end apart: 25 -> 11, of which waited for: 21 -> 6; matrix products, arithmetic and copies ran while one was open for 13% -> 26% of each run, Pallas kernels for 0% -> 0%
where the time goes in v1:
time: 1240 us
  waiting for transfers between devices  681 us (55%)
  matrix products  242 us (20%)
  blocking collectives  132 us (11%)
  local copies, waits for them, and re-layouts  79 us (6%)
  other arithmetic  69 us (6%)
  starting transfers between devices  18.4 us (1%)
  between operations  15.4 us (1%)
    reduce_scatter x4, waiting for transfers between devices, scatter_sum(): lax.psum_scatter(total, ('dp', 'fsdp'), scatter_dimension=0, tiled=True)  457 us
    psum x1, blocking collectives, body(): lax.psum((square_sums, jnp.sum(valid_rows)), ('dp', 'fsdp'))  132 us
    all_to_all x3, waiting for transfers between devices, swap_rows(): lax.all_to_all(split, 'fsdp', split_axis=1, concat_axis=1, tiled=True)  114 us
    all_gather x4, waiting for transfers between devices, gather_rows(): return lax.all_gather(shard, ('dp', 'fsdp'), axis=0, tiled=True)  110 us
    dot_general x4, matrix products, against(): lax.dot_general(grad_rows, matrix, (((1,), (1,)), ((), ())), preferred_el...  64.8 us
    dot_general x4, matrix products, matmul(): return jnp.dot(left, right, preferred_element_type=jnp.float32)  58.5 us
    dot_general x4, matrix products, outer_sum(): lax.dot_general(left, right, (((0,), (0,)), ((), ())), preferred_element_...  50.2 us
  transfers between devices with their start and end apart: 11, of which 6 were waited for; matrix products, arithmetic and copies ran while one was open for 26% of the time, Pallas kernels for 0%

profile of v1, /device:TPU:0, one launch (start us, length us, event | category | flops | bytes accessed | tf_op | source)
XLA Modules:
  0.0 1237.3 jit_solution(10131243089084982970)
XLA Ops:
  14.5 7.3 all-to-all-start
  21.8 4.8 fusion.11
  29.1 6.1 all-to-all-start.1
  38.9 3.5 multiply_cosine_fusion.1
  42.4 4.4 multiply_exponential_fusion
  48.1 113.7 %all-to-all-done.1 = bf16[2,8,64,2048]{3,2,0,1:T(8,128)(2,1)} async-done(((bf16[2,8,64,2048]{3,2,0,1:T(8,128)(2,1)}), bf16[2,8,64,2048]{3,2,0,1:T(8,128)(2,1)}, u32[]{:S(2)}, u32[]{:S(2)}) %all-to-all-start.1) | async-done | bytes 4194336 | tf_op jit(solution)/shard_map/all_to_all | solution.py:103
  167.0 4.3 multiply_reduce_fusion.8
  171.4 5.4 copy.137
  176.8 5.3 copy.138
  182.1 13.0 %fusion.31 = f32[1024,4096]{1,0:T(8,128)S(1)} fusion(bf16[1024,4096]{1,0:T(8,128)(2,1)} %all-gather.5.cloned.1.call-done, f32[1024,1024]{0,1:T(8,128)} %copy.137, f32[1024]{0:T(1024)S(1)} %bitcast.141), kind=kOutput, calls=%fused_computation.93 | convolution fusion | flops 8592031744 | bytes 29364224 | tf_op jit(solution)/shard_map/dot_general | solution.py:48
  205.3 10.4 fusion
  215.7 8.2 multiply_reduce_fusion.7
  223.9 5.3 copy.136
  229.2 4.4 multiply_convert_fusion.5
  233.6 8.7 multiply_reduce_fusion.6
  242.3 61.8 %all-gather.9.cloned.1.call-done = bf16[1024,5632]{1,0:T(8,128)(2,1)} async-done(((bf16[32,5632]{1,0:T(8,128)(2,1)}), bf16[1024,5632]{1,0:T(8,128)(2,1)}) %all-gather.9.cloned.1.call-update) | async-done | bytes 11534352 | tf_op jit(solution)/shard_map/all_gather | solution.py:108
  304.1 20.8 %fusion.32 = f32[1024,5632]{1,0:T(8,128)} fusion(bf16[1024,5632]{1,0:T(8,128)(2,1)} %all-gather.9.cloned.1.call-done, f32[1024,1024]{0,1:T(8,128)} %get-tuple-element.20, f32[1024]{0:T(1024)S(1)} %add_rsqrt_fusion), kind=kOutput, calls=%fused_computation.94 | convolution fusion | flops 11813257216 | bytes 38801408 | tf_op jit(solution)/shard_map/dot_general | solution.py:48
  325.0 47.9 %all-gather.11.cloned.1.call-done = bf16[2816,1024]{1,0:T(8,128)(2,1)} async-done(((bf16[88,1024]{1,0:T(8,128)(2,1)}), bf16[2816,1024]{1,0:T(8,128)(2,1)}) %all-gather.11.cloned.1.call-update) | async-done | bytes 5767184 | tf_op jit(solution)/shard_map/all_gather | solution.py:108
  372.9 20.7 %multiply_convert_fusion.1 = (bf16[1024,2816]{1,0:T(8,128)(2,1)}, bf16[1024,2816]{1,0:T(8,128)(2,1)}, bf16[1024,2816]{1,0:T(8,128)(2,1)}) fusion(f32[1024,5632]{1,0:T(8,128)} %fusion.32, bf16[2816,1024]{1,0:T(8,128)(2,1)} %all-gather.11.cloned.1.call-done, f32[1024,1024]{0,1:T(8,128)} %copy.138, f32[1024]{0:T(1024)S(1)} %bitcast.145), kind=kOutput, calls=%fused_computation.6 | convolution fusion | flops 5924978688 | bytes 50335744 | tf_op jit(solution)/shard_map/dot_general | solution.py:36
  393.6 19.8 %fusion.2 = f32[1024,1024]{0,1:T(8,128)} fusion(bf16[1024,5632]{1,0:T(8,128)(2,1)} %all-gather.9.cloned.1.call-done, bf16[1024,2816]{1,0:T(8,128)(2,1)} %get-tuple-element.22, bf16[1024,2816]{1,0:T(8,128)(2,1)} %get-tuple-element.21), kind=kOutput, calls=%fused_computation.12 | convolution fusion | flops 11834228736 | bytes 27262976 | tf_op jit(solution)/shard_map/dot_general | solution.py:36
  413.4 16.0 %multiply_reduce_fusion.2 = (f32[]{:T(128)}, f32[]{:T(128)}, f32[1024]{0:T(1024)S(1)}, f32[]{:T(128)}, bf16[1024,1024]{0,1:T(8,128)(2,1)}) fusion(f32[1024]{0:T(1024)S(1)} %bitcast.146, f32[1024,1024]{0,1:T(8,128)S(1)} %copy-done.8, f32[1024,1024]{0,1:T(8,128)} %fusion.2, f32[1024]{0:T(1024)S(1)} %add_rsqrt_fusion, f32[1024,1024]{0,1:T(8,128)} %get-tuple-element.58, ...), kind=kOutput, calls=%fused_computation.35 | convolution fusion | flops 5920259072 | bytes 26226700 | tf_op jit(solution)/shard_map/dot_general | solution.py:48
  429.3 3.8 multiply_add_fusion
  435.1 3.7 convolution_convert_fusion.5
  438.8 11.4 convolution_convert_fusion.2
  450.9 3.1 multiply_cosine_fusion
  454.1 8.4 multiply_reduce_fusion.4
  462.5 4.3 fusion.16
  468.8 3.0 copy.146
  471.8 8.5 fusion.1
  480.3 10.3 convolution_bitcast_fusion
  490.6 10.4 copy.145
  501.0 10.4 convolution_bitcast_fusion.1
  511.4 10.3 copy.143
  521.7 6.0 convert_bitcast_fusion
  527.7 3.2 copy.147
  532.8 6.5 fusion.6
  539.4 7.6 fusion.4
  547.0 14.9 %convolution_convert_fusion.1 = bf16[1024,4096]{1,0:T(8,128)(2,1)} fusion(bf16[1024,1024]{1,0:T(8,128)(2,1)} %get-tuple-element.30, bf16[1024,1024]{1,0:T(8,128)(2,1)} %bitcast.134, bf16[1024,1024]{1,0:T(8,128)(2,1)} %get-tuple-element.25, bf16[1024,1024]{1,0:T(8,128)(2,1)S(1)} %get-tuple-element.24, f32[1024,1024]{0,1:T(8,128)} %copy.137, ...), kind=kOutput, calls=%fused_computation.11 | convolution fusion | flops 8629780480 | bytes 20975616 | tf_op jit(solution)/shard_map/dot_general | solution.py:42
  562.0 20.2 %convolution_convert_fusion = bf16[1024,5632]{1,0:T(8,128)(2,1)} fusion(bf16[1024,2816]{1,0:T(8,128)(2,1)} %get-tuple-element.22, bf16[1024,2816]{1,0:T(8,128)(2,1)} %get-tuple-element.21, f32[1024,1024]{0,1:T(8,128)} %get-tuple-element.20, f32[1024]{0:T(1024)S(1)} %add_rsqrt_fusion), kind=kOutput, calls=%fused_computation.8 | convolution fusion | flops 11842093056 | bytes 27267072 | tf_op jit(solution)/shard_map/dot_general | solution.py:42
  582.2 15.9 %multiply_reduce_fusion.3 = (f32[1024]{0:T(1024)S(1)}, f32[1024,1024]{0,1:T(8,128)}) fusion(f32[1024,1024]{0,1:T(8,128)} %copy.137, f32[1024]{0:T(1024)S(1)} %bitcast.143, bf16[1024,4096]{1,0:T(8,128)(2,1)} %all-gather.5.cloned.1.call-done, bf16[1024,1024]{1,0:T(8,128)(2,1)} %get-tuple-element.30, bf16[1024,1024]{1,0:T(8,128)(2,1)} %bitcast.135, ...), kind=kOutput, calls=%fused_computation.37 | convolution fusion | flops 8626633728 | bytes 25174016 | tf_op jit(solution)/shard_map/dot_general | solution.py:36
  598.1 4.0 add_convert_fusion
  604.6 6.7 copy.157
  611.2 4.6 convolution_convert_fusion.4
  618.2 4.7 all-to-all-start.2
  625.6 132.4 %all-reduce = (f32[3]{0:T(128)S(1)}, f32[]{:T(128)}) all-reduce(f32[3]{0:T(128)S(1)} %pad_maximum_fusion.15, f32[]{:T(128)} %fusion.36), channel_id=1, replica_groups=mesh['dp'=4,'fsdp'=8] {'dp','fsdp'}, use_global_device_ids=true, to_apply=%region_18.19 | all-reduce | flops 4 | bytes 32 | tf_op jit(solution)/shard_map/psum | solution.py:250
  768.4 21.1 %reduce-scatter.11.cloned.1.call-done = bf16[88,1024]{1,0:T(8,128)(2,1)} async-done(((bf16[2816,1024]{1,0:T(8,128)(2,1)}), bf16[88,1024]{1,0:T(8,128)(2,1)}) %reduce-scatter.11.cloned.1.call-update) | async-done | bytes 180240 | tf_op jit(solution)/shard_map/reduce_scatter | solution.py:112
  791.1 184.8 %reduce-scatter.5.cloned.1.call-done = bf16[32,4096]{1,0:T(8,128)(2,1)} async-done(((bf16[1024,4096]{1,0:T(8,128)(2,1)}), bf16[32,4096]{1,0:T(8,128)(2,1)}) %reduce-scatter.5.cloned.1.call-update) | async-done | bytes 262160 | tf_op jit(solution)/shard_map/reduce_scatter | solution.py:112
  977.7 250.7 %reduce-scatter.9.cloned.1.call-done = bf16[32,5632]{1,0:T(8,128)(2,1)} async-done(((bf16[1024,5632]{1,0:T(8,128)(2,1)}), bf16[32,5632]{1,0:T(8,128)(2,1)}) %reduce-scatter.9.cloned.1.call-update) | async-done | bytes 360464 | tf_op jit(solution)/shard_map/reduce_scatter | solution.py:112
  (136 shorter events, 59.2 us)
Async XLA Ops:
  7.2 174.9 %all-gather.5.cloned.1.call-start = ((), (), s32[]{:S(2)}) async-start(), calls=%async_computation.7 | async-start | bytes 8650752 | tf_op jit(solution)/shard_map/all_gather | solution.py:108
  8.9 224.7 %all-gather.7.cloned.1.call-start = ((), (), s32[]{:S(2)}) async-start(), calls=%async_computation.8 | async-start | bytes 2162688 | tf_op jit(solution)/shard_map/all_gather | solution.py:108
  9.7 294.5 %all-gather.9.cloned.1.call-start = ((), (), s32[]{:S(2)}) async-start(), calls=%async_computation.9 | async-start | bytes 11894784 | tf_op jit(solution)/shard_map/all_gather | solution.py:108
  12.5 14.0 %copy-start.19 = (s32[2,512]{1,0:T(2,128)}, s32[2,512]{1,0:T(2,128)S(1)}, u32[]{:S(2)}) copy-start(s32[2,512]{1,0:T(2,128)S(1)} %convert_reduce_fusion) | copy-start | bytes 12292
  14.5 14.7 %all-to-all-start = ((s32[8,1,128]{2,1,0:T(1,128)}), s32[8,1,128]{2,1,0:T(1,128)S(1)}, u32[]{:S(2)}, u32[]{:S(2)}) async-start(s32[8,1,128]{2,1,0:T(1,128)} %reshape.334), calls=%async_computation | async-start | bytes 8192 | tf_op jit(solution)/shard_map/all_to_all | solution.py:103
  29.1 6.8 copy-start.24
  29.1 132.7 %all-to-all-start.1 = ((bf16[2,8,64,2048]{3,2,0,1:T(8,128)(2,1)}), bf16[2,8,64,2048]{3,2,0,1:T(8,128)(2,1)}, u32[]{:S(2)}, u32[]{:S(2)}) async-start(bf16[2,8,64,2048]{3,2,0,1:T(8,128)(2,1)} %copy.126), calls=%async_computation.1 | async-start | bytes 8388608 | tf_op jit(solution)/shard_map/all_to_all | solution.py:103
  35.3 337.6 %all-gather.11.cloned.1.call-start = ((), (), s32[]{:S(2)}) async-start(), calls=%async_computation.10 | async-start | bytes 5947392 | tf_op jit(solution)/shard_map/all_gather | solution.py:108
  35.8 723.3 %reduce-scatter.7.cloned.1.call-start = ((), (), s32[]{:S(2)}) async-start(), calls=%async_computation.12 | async-start | bytes 2162688 | tf_op jit(solution)/shard_map/reduce_scatter | solution.py:112
  36.3 0.5 copy-start.27
  36.4 10.4 copy-start.25
  48.1 116.3 %copy-start.22 = (s32[2,512]{1,0:T(2,128)}, s32[2,512]{1,0:T(2,128)S(1)}, u32[]{:S(2)}) copy-start(s32[2,512]{1,0:T(2,128)S(1)} %eq.50) | copy-start | bytes 12292
  176.8 5.4 copy-start.17
  195.1 6.0 copy-start.1
  201.1 1.1 copy-start.13
  201.1 1.2 copy-start.14
  202.2 13.4 %copy-start.5 = (bf16[128,8,8,128]{3,2,1,0:T(8,128)(2,1)}, bf16[128,8,8,128]{3,2,1,0:T(8,128)(2,1)S(1)}, u32[]{:S(2)}) copy-start(bf16[128,8,8,128]{3,2,1,0:T(8,128)(2,1)S(1)} %copy.159) | copy-start | bytes 6291460
  205.3 10.4 copy-start.6
  205.3 10.4 copy-start.7
  393.6 19.8 %copy-start.8 = (f32[1024,1024]{0,1:T(8,128)S(1)}, f32[1024,1024]{0,1:T(8,128)}, u32[]{:S(2)}) copy-start(f32[1024,1024]{0,1:T(8,128)} %get-tuple-element.20) | copy-start | bytes 12582916
  413.4 16.0 %copy-start.9 = (f32[1024,1024]{0,1:T(8,128)S(1)}, f32[1024,1024]{0,1:T(8,128)}, u32[]{:S(2)}) copy-start(f32[1024,1024]{0,1:T(8,128)} %copy.138) | copy-start | bytes 12582916
  433.1 2.0 copy-start.3
  438.8 350.7 %reduce-scatter.11.cloned.1.call-start = ((), (), s32[]{:S(2)}) async-start(), calls=%async_computation.14 | async-start | bytes 5947392 | tf_op jit(solution)/shard_map/reduce_scatter | solution.py:112
  450.3 0.7 copy-start.21
  450.3 0.7 copy-start.26
  450.3 3.8 copy-start.10
  450.3 525.7 %reduce-scatter.5.cloned.1.call-start = ((), (), s32[]{:S(2)}) async-start(), calls=%async_computation.11 | async-start | bytes 8650752 | tf_op jit(solution)/shard_map/reduce_scatter | solution.py:112
  454.1 8.4 copy-start
  466.8 5.0 copy-start.11
  527.7 5.1 copy-start.15
  539.3 7.6 copy-start.18
  547.0 14.9 %copy-start.12 = (bf16[1024,1024]{1,0:T(8,128)(2,1)}, bf16[1024,1024]{1,0:T(8,128)(2,1)S(1)}, u32[]{:S(2)}) copy-start(bf16[1024,1024]{1,0:T(8,128)(2,1)S(1)} %get-tuple-element.24) | copy-start | bytes 6291460
  561.9 666.5 %reduce-scatter.9.cloned.1.call-start = ((), (), s32[]{:S(2)}) async-start(), calls=%async_computation.13 | async-start | bytes 11894784 | tf_op jit(solution)/shard_map/reduce_scatter | solution.py:112
  582.2 15.9 %copy-start.2 = (f32[1024,1024]{0,1:T(8,128)S(1)}, f32[1024,1024]{0,1:T(8,128)}, u32[]{:S(2)}) copy-start(f32[1024,1024]{0,1:T(8,128)} %copy.137) | copy-start | bytes 12582916
  582.2 15.9 %copy-start.4 = (f32[1024,1024]{0,1:T(8,128)S(1)}, f32[1024,1024]{0,1:T(8,128)}, u32[]{:S(2)}) copy-start(f32[1024,1024]{0,1:T(8,128)} %copy-done.3) | copy-start | bytes 12582916
  598.1 4.0 copy-start.16
  604.6 6.7 copy-start.23
  618.2 4.7 copy-start.28
  618.2 142.5 %all-to-all-start.2 = ((bf16[2,8,64,2048]{3,2,0,1:T(8,128)(2,1)}), bf16[2,8,64,2048]{3,2,0,1:T(8,128)(2,1)}, u32[]{:S(2)}, u32[]{:S(2)}) async-start(bf16[2,8,64,2048]{3,2,0,1:T(8,128)(2,1)} %copy.150), calls=%async_computation.2 | async-start | bytes 8388608 | tf_op jit(solution)/shard_map/all_to_all | solution.py:103
  760.7 2.8 copy-start.20
Sparse Core Ops, SparseCore 0:
  11.5 142.0 all-gather.4
  156.6 54.5 all-gather.6
  214.7 89.4 all-gather.8
  306.9 65.9 all-gather.10
  438.9 137.7 reduce-scatter.6
  578.8 210.5 reduce-scatter.10
  791.7 184.1 reduce-scatter.4
  978.3 250.0 reduce-scatter.8
